TPU v7x, 32 devices: a whole 2x2x4 slice. The times are simulated.
32 devices in a mesh: shard: 2 (over y), ctx: 4 (over z), tp: 4 (over x, core).
Axes of the slice: x: 2, y: 2, z: 4, core: 2. Of those that a mesh axis runs over, the one named last changes fastest.
Arguments:
- inputs: bfloat16 [4, 1024, 768], P('shard', ('ctx', 'tp')), may hold values from -6 to 6
- seg_ids: int32 [4, 1024], P('shard', 'ctx'), may hold values from 0 to 7, never falling along the last dimension, each value on 1 to 512 neighbouring positions
- feature_map: float32 [12, 64, 256], P('tp'), may hold values from -6 to 6
- w_query: bfloat16 [768, 768], P(('shard', 'ctx'), 'tp'), may hold values from -0.21875 to 0.21875
- w_key: bfloat16 [768, 768], P(('shard', 'ctx'), 'tp'), may hold values from -0.21875 to 0.21875
- w_value: bfloat16 [768, 768], P(('shard', 'ctx'), 'tp'), may hold values from -0.21875 to 0.21875
- w_out: bfloat16 [768, 768], P('tp', ('shard', 'ctx')), may hold values from -0.875 to 0.875
- gain_attn: float32 [768], replicated, may hold values from 0.5 to 1.5
- shift_attn: float32 [768], replicated, may hold values from -3 to 3
- w_up: bfloat16 [768, 3072], P(('shard', 'ctx'), 'tp'), may hold values from -0.21875 to 0.21875
- bias_up: float32 [3072], P('tp'), may hold values from -3 to 3
- w_down: bfloat16 [3072, 768], P('tp', ('shard', 'ctx')), may hold values from -0.109375 to 0.109375
- bias_down: float32 [768], replicated, may hold values from -3 to 3
- gain_ffn: float32 [768], replicated, may hold values from 0.5 to 1.5
- shift_ffn: float32 [768], replicated, may hold values from -3 to 3
- cotangent: bfloat16 [4, 1024, 768], P('shard', ('ctx', 'tp')), may hold values from -6 to 6
Outputs:
- outputs: bfloat16 [4, 1024, 768], P('shard', ('ctx', 'tp'))
- grad_inputs: bfloat16 [4, 1024, 768], P('shard', ('ctx', 'tp'))
- grad_query: float32 [768, 768], P(('shard', 'ctx'), 'tp')
- grad_key: float32 [768, 768], P(('shard', 'ctx'), 'tp')
- grad_value: float32 [768, 768], P(('shard', 'ctx'), 'tp')
- grad_out: float32 [768, 768], P('tp', ('shard', 'ctx'))
- grad_gain_attn: float32 [768], replicated
- grad_shift_attn: float32 [768], replicated
- grad_up: float32 [768, 3072], P(('shard', 'ctx'), 'tp')
- grad_bias_up: float32 [3072], P('tp')
- grad_down: float32 [3072, 768], P('tp', ('shard', 'ctx'))
- grad_bias_down: float32 [768], replicated
- grad_gain_ffn: float32 [768], replicated
- grad_shift_ffn: float32 [768], replicated
Inputs may be any that keep to these rules, and one draw needn't show every extreme that they name: `seg_ids`: within each sequence the numbers never fall, every number below 8 occurs, and no document has more than 512 tokens.
All inputs are finite; a program needn't handle non-finite values.
Results may differ from a plain program's by a relative error of at most 0.025.
Values may be sent and summed in bfloat16 or wider, within the bound.
A program may use at most 128 MiB of HBM per device.

v0:
```python
import jax
import jax.numpy as jnp
from jax import lax
from jax.sharding import PartitionSpec as P

HEAD_DIM = 64
FEATS = 256
FF = 3072
SEGS = 8
highest = lax.Precision.HIGHEST
root_half = 0.7071067811865476
inv_root_tau = 0.3989422804014327
norm_eps = 1e-05


def gelu_value(upper):
    return upper * 0.5 * (1.0 + lax.erf(upper * root_half))


def gelu_slope(upper):
    return 0.5 * (1.0 + lax.erf(upper * root_half)) + upper * inv_root_tau * jnp.exp(
        -0.5 * upper * upper
    )


def layer_norm(hidden_in, gain_vec, shift_vec):
    mean_val = jnp.mean(hidden_in, -1, keepdims=True)
    centred = hidden_in - mean_val
    inv_std = lax.rsqrt(jnp.mean(centred * centred, -1, keepdims=True) + norm_eps)
    normed = centred * inv_std
    return (normed * gain_vec + shift_vec, normed, inv_std)


def norm_back(grad_in, normed, inv_std, gain_vec):
    scaled = grad_in * gain_vec
    grad_hidden = inv_std * (
        scaled
        - jnp.mean(scaled, -1, keepdims=True)
        - normed * jnp.mean(scaled * normed, -1, keepdims=True)
    )
    return (grad_hidden, jnp.sum(grad_in * normed, (0, 1)), jnp.sum(grad_in, (0, 1)))


def features(projected, omega_local):
    seq_count, ctx_rows, width = projected.shape
    heads_here = omega_local.shape[0]
    scaled = projected.reshape(seq_count, ctx_rows, heads_here, HEAD_DIM) * HEAD_DIM ** (-0.25)
    angles = jnp.einsum("schd,hdm->schm", scaled, omega_local, precision=highest)
    squares = 0.5 * jnp.sum(scaled * scaled, -1, keepdims=True)
    return (jnp.exp(angles - squares) * FEATS ** (-0.5), scaled)


def feature_back(grad_phi, phi_full, scaled, omega_local):
    grad_angle = grad_phi * phi_full
    grad_scaled = jnp.einsum("schm,hdm->schd", grad_angle, omega_local, precision=highest)
    grad_scaled = grad_scaled - scaled * jnp.sum(grad_angle, -1, keepdims=True)
    seq_count, ctx_rows, heads_here, head_width = scaled.shape
    return (grad_scaled * HEAD_DIM ** (-0.25)).reshape(seq_count, ctx_rows, heads_here * head_width)


def spread_rows(mask_low, left):
    ctx_rows, heads_here, feat_count = left.shape
    wide = mask_low[:, None, :, None] * left[:, :, None, :]
    return wide.reshape(ctx_rows, heads_here, -1)


def segment_outer(operands):
    mask_low, left, right = operands
    return jnp.einsum(
        "chx,che->hxe", spread_rows(mask_low, left), right, preferred_element_type=jnp.float32
    )


def segment_apply(operands):
    mask_low, left, table = operands
    return jnp.einsum(
        "chx,hxe->che", spread_rows(mask_low, left), table, preferred_element_type=jnp.float32
    )


def segment_back(operands):
    mask_full, left, table = operands
    ctx_rows, heads_here, width = left.shape
    seg_count = mask_full.shape[1]
    wide = jnp.einsum("che,hxe->chx", left, table, preferred_element_type=jnp.float32)
    wide = wide.reshape(ctx_rows, heads_here, seg_count, -1)
    return jnp.sum(wide * mask_full[:, None, :, None], 2)


def inner_product(left, right):
    return lax.dot_general(
        left, right, (((0,), (0,)), ((), ())), preferred_element_type=jnp.float32
    )


def right_transposed(left, right):
    return lax.dot_general(
        left, right, (((1,), (1,)), ((), ())), preferred_element_type=jnp.float32
    )


def per_device(
    inputs,
    seg_ids,
    feature_map,
    w_query,
    w_key,
    w_value,
    w_out,
    gain_attn,
    shift_attn,
    w_up,
    bias_up,
    w_down,
    bias_down,
    gain_ffn,
    shift_ffn,
    cotangent,
):
    full_query, full_key, full_value, full_up, full_out, full_down = (
        lax.all_gather(w_query, ("shard", "ctx"), axis=0, tiled=True),
        lax.all_gather(w_key, ("shard", "ctx"), axis=0, tiled=True),
        lax.all_gather(w_value, ("shard", "ctx"), axis=0, tiled=True),
        lax.all_gather(w_up, ("shard", "ctx"), axis=0, tiled=True),
        lax.all_gather(w_out, ("shard", "ctx"), axis=1, tiled=True),
        lax.all_gather(w_down, ("shard", "ctx"), axis=1, tiled=True),
    )
    seq_count, row_share, width = inputs.shape
    rows_all = lax.all_gather(inputs, "tp", axis=1, tiled=True)
    ctx_rows = rows_all.shape[1]
    token_count = seq_count * ctx_rows
    flat = rows_all.reshape(token_count, width)
    heads_here = feature_map.shape[0]
    head_cols = heads_here * HEAD_DIM
    query_proj = jnp.dot(flat, full_query, preferred_element_type=jnp.float32).reshape(
        seq_count, ctx_rows, head_cols
    )
    key_proj = jnp.dot(flat, full_key, preferred_element_type=jnp.float32).reshape(
        seq_count, ctx_rows, head_cols
    )
    value_low = jnp.dot(flat, full_value, preferred_element_type=jnp.float32).astype(jnp.bfloat16)
    value_low = value_low.reshape(seq_count, ctx_rows, head_cols)
    value_four = value_low.reshape(seq_count, ctx_rows, heads_here, HEAD_DIM)
    phi_query, scaled_query = features(query_proj, feature_map)
    phi_key, scaled_key = features(key_proj, feature_map)
    phq_low = phi_query.astype(jnp.bfloat16)
    phk_low = phi_key.astype(jnp.bfloat16)
    matches = seg_ids[:, :, None] == jnp.arange(SEGS, dtype=jnp.int32)[None, None, :]
    mask_low = matches.astype(jnp.bfloat16)
    mask_full = matches.astype(jnp.float32)
    kv_part = lax.map(segment_outer, (mask_low, phk_low, value_four))
    z_part = jnp.einsum("scg,schm->shgm", mask_low, phk_low, preferred_element_type=jnp.float32)
    kv_sum, z_sum = lax.psum((kv_part, z_part), "ctx")
    kv_low = kv_sum.astype(jnp.bfloat16)
    numer = lax.map(segment_apply, (mask_low, phq_low, kv_low))
    phq_wide = phq_low.astype(jnp.float32)
    denom = jnp.sum(
        jnp.einsum("schm,shgm->schg", phq_wide, z_sum, precision=highest)
        * mask_full[:, :, None, :],
        -1,
    )
    mixed = numer / denom[..., None]
    mixed_low = mixed.astype(jnp.bfloat16).reshape(seq_count, ctx_rows, head_cols)
    piece = mixed_low
    attn_sum = jnp.swapaxes(
        lax.psum_scatter(
            jnp.einsum("scf,fd->csd", piece, full_out, preferred_element_type=jnp.float32),
            "tp",
            scatter_dimension=0,
            tiled=True,
        ),
        0,
        1,
    )
    first, normed_one, inv_one = layer_norm(
        inputs.astype(jnp.float32) + attn_sum, gain_attn, shift_attn
    )
    first_low = first.astype(jnp.bfloat16)
    first_rows = lax.all_gather(first_low, "tp", axis=1, tiled=True)
    first_flat = first_rows.reshape(token_count, width)
    upper = jnp.dot(first_flat, full_up, preferred_element_type=jnp.float32) + bias_up
    ffn_here = upper.shape[1]
    hidden_low = gelu_value(upper).astype(jnp.bfloat16)
    hidden_three = hidden_low.reshape(seq_count, ctx_rows, ffn_here)
    piece = hidden_three
    branch = jnp.swapaxes(
        lax.psum_scatter(
            jnp.einsum("scf,fd->csd", piece, full_down, preferred_element_type=jnp.float32),
            "tp",
            scatter_dimension=0,
            tiled=True,
        ),
        0,
        1,
    )
    final, normed_two, inv_two = layer_norm(first + branch + bias_down, gain_ffn, shift_ffn)
    outputs = final.astype(jnp.bfloat16)
    full_query, full_key, full_value, full_up, full_out, full_down = (
        lax.all_gather(w_query, ("shard", "ctx"), axis=0, tiled=True),
        lax.all_gather(w_key, ("shard", "ctx"), axis=0, tiled=True),
        lax.all_gather(w_value, ("shard", "ctx"), axis=0, tiled=True),
        lax.all_gather(w_up, ("shard", "ctx"), axis=0, tiled=True),
        lax.all_gather(w_out, ("shard", "ctx"), axis=1, tiled=True),
        lax.all_gather(w_down, ("shard", "ctx"), axis=1, tiled=True),
    )
    grad_final = cotangent.astype(jnp.float32)
    grad_two, grad_gain_ffn, grad_shift_ffn = norm_back(grad_final, normed_two, inv_two, gain_ffn)
    grad_bias_down = jnp.sum(grad_two, (0, 1))
    grad_two_rows = lax.all_gather(grad_two.astype(jnp.bfloat16), "tp", axis=1, tiled=True)
    grad_two_flat = grad_two_rows.reshape(token_count, width)
    grad_hidden = right_transposed(grad_two_flat, full_down)
    grad_upper = (grad_hidden * gelu_slope(upper)).astype(jnp.bfloat16)
    grad_down = inner_product(hidden_low, grad_two_flat)
    grad_up = inner_product(first_flat, grad_upper)
    grad_bias_local = jnp.sum(grad_upper.astype(jnp.float32), 0)
    grad_upper_three = grad_upper.reshape(seq_count, ctx_rows, ffn_here)
    piece = grad_upper_three
    grad_first = grad_two + jnp.swapaxes(
        lax.psum_scatter(
            jnp.einsum("scf,df->csd", piece, full_up, preferred_element_type=jnp.float32),
            "tp",
            scatter_dimension=0,
            tiled=True,
        ),
        0,
        1,
    )
    grad_one, grad_gain_attn, grad_shift_attn = norm_back(
        grad_first, normed_one, inv_one, gain_attn
    )
    grad_one_rows = lax.all_gather(grad_one.astype(jnp.bfloat16), "tp", axis=1, tiled=True)
    grad_one_flat = grad_one_rows.reshape(token_count, width)
    grad_out = inner_product(mixed_low.reshape(token_count, head_cols), grad_one_flat)
    grad_mixed = right_transposed(grad_one_flat, full_out).reshape(
        seq_count, ctx_rows, heads_here, HEAD_DIM
    )
    grad_numer = (grad_mixed / denom[..., None]).astype(jnp.bfloat16)
    grad_denom = -jnp.sum(grad_mixed * mixed, -1) / denom
    kv_grad_part = lax.map(segment_outer, (mask_low, phq_low, grad_numer))
    z_grad_part = jnp.einsum(
        "scg,schm->shgm", mask_full, phq_wide * grad_denom[..., None], precision=highest
    )
    kv_grad, z_grad = (
        lax.psum(kv_grad_part.astype(jnp.bfloat16), "ctx").astype(jnp.float32),
        lax.psum(z_grad_part.astype(jnp.bfloat16), "ctx").astype(jnp.float32),
    )
    kv_grad_low = kv_grad.astype(jnp.bfloat16)
    grad_phq = lax.map(segment_back, (mask_full, grad_numer, kv_low))
    grad_phq = grad_phq + grad_denom[..., None] * jnp.einsum(
        "scg,shgm->schm", mask_full, z_sum, precision=highest
    )
    grad_phk = lax.map(segment_back, (mask_full, value_four, kv_grad_low))
    grad_phk = grad_phk + jnp.einsum("scg,shgm->schm", mask_full, z_grad, precision=highest)
    grad_value_rows = lax.map(segment_apply, (mask_low, phk_low, kv_grad_low)).astype(jnp.bfloat16)
    grad_value_rows = grad_value_rows.reshape(seq_count, ctx_rows, head_cols)
    grad_query_rows = feature_back(grad_phq, phi_query, scaled_query, feature_map).astype(
        jnp.bfloat16
    )
    grad_key_rows = feature_back(grad_phk, phi_key, scaled_key, feature_map).astype(jnp.bfloat16)
    grad_query = inner_product(flat, grad_query_rows.reshape(token_count, head_cols))
    grad_key = inner_product(flat, grad_key_rows.reshape(token_count, head_cols))
    grad_value = inner_product(flat, grad_value_rows.reshape(token_count, head_cols))
    total = jnp.einsum(
        "scf,df->csd", grad_query_rows, full_query, preferred_element_type=jnp.float32
    )
    total = total + jnp.einsum(
        "scf,df->csd", grad_key_rows, full_key, preferred_element_type=jnp.float32
    )
    grad_rows = jnp.swapaxes(
        lax.psum_scatter(
            (
                total
                + jnp.einsum(
                    "scf,df->csd", grad_value_rows, full_value, preferred_element_type=jnp.float32
                )
            ).astype(jnp.bfloat16),
            "tp",
            scatter_dimension=0,
            tiled=True,
        ).astype(jnp.float32),
        0,
        1,
    )
    grad_inputs = (grad_one + grad_rows).astype(jnp.bfloat16)
    grad_query, grad_key, grad_value, grad_up, grad_out, grad_down = (
        lax.psum_scatter(grad_query, ("shard", "ctx"), scatter_dimension=0, tiled=True),
        lax.psum_scatter(grad_key, ("shard", "ctx"), scatter_dimension=0, tiled=True),
        lax.psum_scatter(grad_value, ("shard", "ctx"), scatter_dimension=0, tiled=True),
        lax.psum_scatter(grad_up, ("shard", "ctx"), scatter_dimension=0, tiled=True),
        lax.psum_scatter(grad_out, ("shard", "ctx"), scatter_dimension=1, tiled=True),
        lax.psum_scatter(grad_down, ("shard", "ctx"), scatter_dimension=1, tiled=True),
    )
    tp_index = lax.axis_index("tp")
    padded_bias = lax.dynamic_update_slice(
        jnp.zeros((FF,), jnp.float32), grad_bias_local, (tp_index * ffn_here,)
    )
    grad_gain_attn, grad_shift_attn, grad_gain_ffn, grad_shift_ffn, grad_bias_down, padded_bias = (
        lax.psum(
            (
                grad_gain_attn,
                grad_shift_attn,
                grad_gain_ffn,
                grad_shift_ffn,
                grad_bias_down,
                padded_bias,
            ),
            ("shard", "ctx", "tp"),
        )
    )
    grad_bias_up = lax.dynamic_slice(padded_bias, (tp_index * ffn_here,), (ffn_here,))
    return (
        outputs,
        grad_inputs,
        grad_query,
        grad_key,
        grad_value,
        grad_out,
        grad_gain_attn,
        grad_shift_attn,
        grad_up,
        grad_bias_up,
        grad_down,
        grad_bias_down,
        grad_gain_ffn,
        grad_shift_ffn,
    )


def solution(mesh):
    placed = (
        P("shard", ("ctx", "tp"), None),
        P("shard", "ctx"),
        P("tp", None, None),
        P(("shard", "ctx"), "tp"),
        P(("shard", "ctx"), "tp"),
        P(("shard", "ctx"), "tp"),
        P("tp", ("shard", "ctx")),
        P(),
        P(),
        P(("shard", "ctx"), "tp"),
        P("tp"),
        P("tp", ("shard", "ctx")),
        P(),
        P(),
        P(),
        P("shard", ("ctx", "tp"), None),
    )
    return jax.shard_map(
        per_device,
        mesh=mesh,
        in_specs=placed,
        out_specs=(
            P("shard", ("ctx", "tp"), None),
            P("shard", ("ctx", "tp"), None),
            P(("shard", "ctx"), "tp"),
            P(("shard", "ctx"), "tp"),
            P(("shard", "ctx"), "tp"),
            P("tp", ("shard", "ctx")),
            P(),
            P(),
            P(("shard", "ctx"), "tp"),
            P("tp"),
            P("tp", ("shard", "ctx")),
            P(),
            P(),
            P(),
        ),
        check_vma=False,
    )
```

profile of v0, /device:TPU:0, one launch (start us, length us, event | category | flops | bytes accessed | tf_op | source)
XLA Modules:
  0.0 1010.8 jit_solution(17872332154931087539)
XLA Ops:
  8.1 10.4 %all_gather.36 = bf16[2,256,768]{2,1,0:T(8,128)(2,1)S(1)} all-gather(bf16[2,64,768]{2,1,0:T(8,128)(2,1)} %param.28), channel_id=1, replica_groups=mesh['shard'=2,'ctx'=4,'tp'=4] {'tp'}, dimensions={1}, use_global_device_ids=true | all-gather | bytes 983040 | tf_op jit(solution)/shard_map/all_gather | solution.py:129
  18.5 32.5 %all_gather.37 = bf16[768,192]{1,0:T(8,128)(2,1)S(1)} all-gather(bf16[96,192]{1,0:T(8,128)(2,1)} %param.32), channel_id=1, replica_groups=mesh['shard'=2,'ctx'=4,'tp'=4] {'shard','ctx'}, dimensions={0}, use_global_device_ids=true | all-gather | bytes 331776 | tf_op jit(solution)/shard_map/all_gather | solution.py:122
  52.3 2.7 fusion.159
  56.2 31.6 %all_gather.38 = bf16[768,192]{1,0:T(8,128)(2,1)S(1)} all-gather(bf16[96,192]{1,0:T(8,128)(2,1)S(1)} %copy-done.48), channel_id=1, replica_groups=mesh['shard'=2,'ctx'=4,'tp'=4] {'shard','ctx'}, dimensions={0}, use_global_device_ids=true | all-gather | bytes 331776 | tf_op jit(solution)/shard_map/all_gather | solution.py:123
  90.6 2.1 convolution_bitcast_fusion.8
  92.7 20.8 %while.66 = (s32[]{:T(128)}, f32[2,3,2048,64]{2,3,1,0:T(8,128)}, bf16[2,256,8]{2,1,0:T(8,128)(2,1)S(1)}, bf16[2,256,3,256]{3,1,2,0:T(8,128)(2,1)}, bf16[2,256,3,64]{1,3,2,0:T(8,128)(2,1)}) while((s32[]{:T(128)}, f32[2,3,2048,64]{2,3,1,0:T(8,128)}, bf16[2,256,8]{2,1,0:T(8,128)(2,1)S(1)}, bf16[2,256,3,256]{3,1,2,0:T(8,128)(2,1)}, ...), condition=%wide.region_3.4_spmd.clone, body=%wide.region_2.3_spmd.sunk.clone | while | flops 207618048 | bytes 20427872 | solution.py:151
  93.7 2.2 mul.739
  95.9 4.2 mul.740
  101.1 2.1 fusion.233
  104.2 2.2 mul.739
  106.4 4.2 mul.740
  111.5 2.0 fusion.233
  113.6 32.0 %all_gather.39 = bf16[768,192]{1,0:T(8,128)(2,1)S(1)} all-gather(bf16[96,192]{1,0:T(8,128)(2,1)S(1)} %copy-done.49), channel_id=1, replica_groups=mesh['shard'=2,'ctx'=4,'tp'=4] {'shard','ctx'}, dimensions={0}, use_global_device_ids=true | all-gather | bytes 331776 | tf_op jit(solution)/shard_map/all_gather | solution.py:121
  145.7 2.3 broadcast_multiply_fusion
  148.0 2.7 fusion.160
  152.0 96.4 %all-reduce.6 = (bf16[2,3,2048,64]{2,3,1,0:T(8,128)(2,1)}, f32[2,3,8,256]{3,2,1,0:T(8,128)S(1)}) all-reduce(f32[2,3,2048,64]{2,3,1,0:T(8,128)} %get-tuple-element.176, f32[2,3,8,256]{3,2,1,0:T(8,128)S(1)} %copy-done.46), channel_id=1, replica_groups=mesh['shard'=2,'ctx'=4,'tp'=4] {'ctx'}, use_global_device_ids=true, to_apply=%region_4.5 | all-reduce | flops 798720 | bytes 4816896 | tf_op jit(solution)/shard_map/psum | solution.py:153
  248.4 19.4 %while.67 = (s32[]{:T(128)}, f32[2,256,3,64]{1,3,2,0:T(8,128)}, bf16[2,3,2048,64]{2,3,1,0:T(8,128)(2,1)}, bf16[2,256,8]{2,1,0:T(8,128)(2,1)S(1)}, bf16[2,256,3,256]{3,1,2,0:T(8,128)(2,1)}) while((s32[]{:T(128)}, f32[2,256,3,64]{1,3,2,0:T(8,128)}, bf16[2,3,2048,64]{2,3,1,0:T(8,128)(2,1)}, bf16[2,256,8]{2,1,0:T(8,128)(2,1)S(1)}, ...), condition=%wide.region_6.7_spmd.clone, body=%wide.region_5.6_spmd.sunk.clone | while | flops 202899456 | bytes 31536224 | solution.py:155
  249.9 3.5 mul.745
  255.2 2.9 fusion.236
  259.6 3.5 mul.745
  264.9 2.9 fusion.236
  268.7 31.8 %all_gather.40 = bf16[192,768]{0,1:T(8,128)(2,1)S(1)} all-gather(bf16[192,96]{0,1:T(8,128)(2,1)S(1)} %copy.105), channel_id=1, replica_groups=mesh['shard'=2,'ctx'=4,'tp'=4] {'shard','ctx'}, dimensions={1}, use_global_device_ids=true | all-gather | bytes 331776 | tf_op jit(solution)/shard_map/all_gather | solution.py:125
  300.6 1.9 fusion.106
  305.4 27.2 %reduce-scatter.19.cloned.1.call-done = f32[64,2,768]{2,0,1:T(8,128)} async-done(((f32[256,2,768]{2,0,1:T(8,128)}), f32[64,2,768]{2,0,1:T(8,128)}) %reduce-scatter.19.cloned.1.call-update) | async-done | bytes 393232 | tf_op jit(solution)/shard_map/reduce_scatter | solution.py:166
  334.7 8.0 all_gather.41
  342.7 5.8 all-gather.3.cloned.1.call-done
  348.4 3.3 multiply_convert_fusion
  351.7 38.5 %all-gather.5.cloned.1.call-done = bf16[768,768]{0,1:T(8,128)(2,1)} async-done(((bf16[768,96]{0,1:T(8,128)(2,1)}), bf16[768,768]{0,1:T(8,128)(2,1)}) %all-gather.5.cloned.1.call-update) | async-done | bytes 1179664 | tf_op jit(solution)/shard_map/all_gather | solution.py:126
  390.2 3.3 convolution_bitcast_fusion.2
  393.6 26.5 %reduce-scatter.21.cloned.1.call-done = f32[64,2,768]{2,0,1:T(8,128)} async-done(((f32[256,2,768]{2,0,1:T(8,128)}), f32[64,2,768]{2,0,1:T(8,128)}) %reduce-scatter.21.cloned.1.call-update) | async-done | bytes 393232 | tf_op jit(solution)/shard_map/reduce_scatter | solution.py:187
  422.0 8.1 all_gather.44
  432.7 2.0 convolution_bitcast_fusion.1
  438.0 25.5 %reduce-scatter.23.cloned.1.call-done = f32[64,2,768]{2,0,1:T(8,128)} async-done(((f32[256,2,768]{2,0,1:T(8,128)}), f32[64,2,768]{2,0,1:T(8,128)}) %reduce-scatter.23.cloned.1.call-update) | async-done | bytes 393232 | tf_op jit(solution)/shard_map/reduce_scatter | solution.py:219
  463.5 2.7 fusion.122
  466.4 8.0 all_gather.45
  476.2 20.0 %while.69 = (s32[]{:T(128)}, bf16[2,3,2048,64]{2,3,1,0:T(8,128)(2,1)}, bf16[2,256,8]{2,1,0:T(8,128)(2,1)S(1)}, bf16[2,256,3,256]{3,1,2,0:T(8,128)(2,1)}, bf16[2,256,3,64]{1,3,2,0:T(8,128)(2,1)}) while((s32[]{:T(128)}, bf16[2,3,2048,64]{2,3,1,0:T(8,128)(2,1)}, bf16[2,256,8]{2,1,0:T(8,128)(2,1)S(1)}, ...), condition=%wide.region_26.27_spmd.clone, body=%wide.region_25.26_spmd.sunk.clone | while | flops 207618048 | bytes 20427872 | solution.py:239
  477.2 2.1 mul.751
  479.2 4.2 mul.752
  487.2 2.1 mul.751
  489.2 4.2 mul.752
  497.8 7.0 while.68
  497.8 2.0 fusion.239
  501.3 1.9 fusion.239
  504.8 2.5 fusion.161
  508.3 20.2 %psum.73 = bf16[2,3,8,256]{3,2,1,0:T(8,128)(2,1)S(1)} all-reduce(bf16[2,3,8,256]{3,2,1,0:T(8,128)(2,1)S(1)} %fusion.107), channel_id=1, replica_groups=mesh['shard'=2,'ctx'=4,'tp'=4] {'ctx'}, use_global_device_ids=true, to_apply=%region_31.32 | all-reduce | flops 12288 | bytes 49152 | tf_op jit(solution)/shard_map/psum | solution.py:245
  532.7 33.9 %all-reduce.5.cloned.1.call-done = bf16[2,3,2048,64]{2,3,1,0:T(8,128)(2,1)} async-done(((bf16[2,3,2048,64]{2,3,1,0:T(8,128)(2,1)}), bf16[2,3,2048,64]{2,3,1,0:T(8,128)(2,1)}) %all-reduce.5.cloned.1.call-update) | async-done | bytes 1572880 | tf_op jit(solution)/shard_map/psum | solution.py:244
  568.0 7.5 while.70
  568.0 2.3 fusion.245
  571.8 2.2 fusion.245
  575.5 2.0 fusion.162
  580.4 19.7 %while.71 = (s32[]{:T(128)}, bf16[2,256,3,64]{1,3,2,0:T(8,128)(2,1)}, bf16[2,3,2048,64]{2,3,1,0:T(8,128)(2,1)}, bf16[2,256,8]{2,1,0:T(8,128)(2,1)S(1)}, bf16[2,256,3,256]{3,1,2,0:T(8,128)(2,1)}) while((s32[]{:T(128)}, bf16[2,256,3,64]{1,3,2,0:T(8,128)(2,1)}, bf16[2,3,2048,64]{2,3,1,0:T(8,128)(2,1)}, ...), condition=%wide.region_34.35_spmd.clone, body=%wide.region_33.34_spmd.sunk.clone | while | flops 202899456 | bytes 33109144 | solution.py:254
  581.9 3.5 mul.759
  587.4 2.2 fusion.248
  591.7 3.5 mul.759
  597.2 2.2 fusion.248
  600.1 3.5 fusion.75
  605.5 2.2 fusion.164
  609.1 2.2 fusion.163
  616.1 40.8 %all-reduce = (f32[768]{0:T(1024)}, f32[768]{0:T(1024)}, f32[3072]{0:T(1024)S(1)}, f32[768]{0:T(1024)}, f32[768]{0:T(1024)}, /*index=5*/f32[768]{0:T(1024)}) all-reduce(f32[768]{0:T(1024)S(1)} %copy-done.69, f32[768]{0:T(1024)S(1)} %copy-done.68, ...), channel_id=1, replica_groups=mesh['shard'=2,'ctx'=4,'tp'=4] {'shard','ctx','tp'}, use_global_device_ids=true, to_apply=%region_41.42 | all-reduce | flops 6912 | bytes 55296 | tf_op jit(solution)/shard_map/psum | solution.py:298
  661.1 63.8 %reduce-scatter.31.cloned.1.call-done = f32[96,192]{1,0:T(8,128)} async-done(((f32[768,192]{1,0:T(8,128)}), f32[96,192]{1,0:T(8,128)}) %reduce-scatter.31.cloned.1.call-update) | async-done | bytes 73744
  724.9 73.0 %reduce-scatter.29.cloned.1.call-done = f32[768,96]{0,1:T(8,128)} async-done(((f32[768,768]{0,1:T(8,128)}), f32[768,96]{0,1:T(8,128)}) %reduce-scatter.29.cloned.1.call-update) | async-done | bytes 294928 | tf_op jit(solution)/shard_map/reduce_scatter | solution.py:291
  797.9 73.1 %reduce-scatter.27.cloned.1.call-done = f32[96,768]{1,0:T(8,128)} async-done(((f32[768,768]{1,0:T(8,128)}), f32[96,768]{1,0:T(8,128)}) %reduce-scatter.27.cloned.1.call-update) | async-done | bytes 294928 | tf_op jit(solution)/shard_map/reduce_scatter | solution.py:289
  871.0 66.2 %reduce-scatter.33.cloned.1.call-done = f32[96,192]{1,0:T(8,128)} async-done(((f32[768,192]{1,0:T(8,128)}), f32[96,192]{1,0:T(8,128)}) %reduce-scatter.33.cloned.1.call-update) | async-done | bytes 73744
  937.2 66.2 %reduce-scatter.35.cloned.1.call-done = f32[96,192]{1,0:T(8,128)} async-done(((f32[768,192]{1,0:T(8,128)}), f32[96,192]{1,0:T(8,128)}) %reduce-scatter.35.cloned.1.call-update) | async-done | bytes 73744
  (326 shorter events, 77.2 us)
Async XLA Ops:
  8.0 44.3 %copy-start = (f32[3,64,256]{2,1,0:T(8,128)S(1)}, f32[3,64,256]{2,1,0:T(8,128)}, u32[]{:S(2)}) copy-start(f32[3,64,256]{2,1,0:T(8,128)} %param.30) | copy-start | bytes 589828
  8.0 324.6 %reduce-scatter.19.cloned.1.call-start = ((), (), s32[]{:S(2)}) async-start(), calls=%async_computation.10 | async-start | bytes 1966080 | tf_op jit(solution)/shard_map/reduce_scatter | solution.py:166
  18.5 69.3 %copy-start.4 = (bf16[2,256,768]{2,1,0:T(8,128)(2,1)}, bf16[2,256,768]{2,1,0:T(8,128)(2,1)S(1)}, u32[]{:S(2)}) copy-start(bf16[2,256,768]{2,1,0:T(8,128)(2,1)S(1)} %all_gather.36) | copy-start | bytes 2359300
  51.0 4.1 copy-start.16
  52.3 3.9 copy-start.48
  56.2 33.5 %copy-start.56 = (s32[2,256]{1,0:T(2,128)S(1)}, s32[2,256]{1,0:T(2,128)}, u32[]{:S(2)}) copy-start(s32[2,256]{1,0:T(2,128)} %param.29) | copy-start | bytes 6148
  92.7 20.8 %copy-start.49 = (bf16[96,192]{1,0:T(8,128)(2,1)S(1)}, bf16[96,192]{1,0:T(8,128)(2,1)}, u32[]{:S(2)}) copy-start(bf16[96,192]{1,0:T(8,128)(2,1)} %param.31) | copy-start | bytes 110596
  145.5 5.2 copy-start.18
  148.0 3.9 copy-start.40
  150.7 97.6 %copy-start.24 = (bf16[2,256,3,256]{1,3,0,2:T(8,128)(2,1)}, bf16[2,256,3,256]{1,3,0,2:T(8,128)(2,1)S(1)}, u32[]{:S(2)}) copy-start(bf16[2,256,3,256]{1,3,0,2:T(8,128)(2,1)S(1)} %get-tuple-element.414) | copy-start | bytes 2359300
  267.8 34.6 %copy-start.45 = (f32[2,256,3,64]{1,3,2,0:T(8,128)S(1)}, f32[2,256,3,64]{1,3,2,0:T(8,128)}, u32[]{:S(2)}) copy-start(f32[2,256,3,64]{1,3,2,0:T(8,128)} %get-tuple-element.177) | copy-start | bytes 1179652
  302.5 30.1 %copy-start.42 = (bf16[2,64,768]{2,1,0:T(8,128)(2,1)S(1)}, bf16[2,64,768]{2,1,0:T(8,128)(2,1)}, u32[]{:S(2)}) copy-start(bf16[2,64,768]{2,1,0:T(8,128)(2,1)} %param.28) | copy-start | bytes 589828
  304.1 30.4 %copy-start.47 = (f32[768]{0:T(1024)S(1)}, f32[768]{0:T(1024)}, u32[]{:S(2)}) copy-start(f32[768]{0:T(1024)} %param.35) | copy-start | bytes 9220
  304.1 30.4 %copy-start.61 = (f32[768]{0:T(1024)S(1)}, f32[768]{0:T(1024)}, u32[]{:S(2)}) copy-start(f32[768]{0:T(1024)} %param.36) | copy-start | bytes 9220
  304.1 44.3 %all-gather.3.cloned.1.call-start = ((), (), s32[]{:S(2)}) async-start(), calls=%async_computation.11 | async-start | bytes 1327104 | tf_op jit(solution)/shard_map/all_gather | solution.py:124
  304.7 85.5 %all-gather.5.cloned.1.call-start = ((), (), s32[]{:S(2)}) async-start(), calls=%async_computation.12 | async-start | bytes 1327104 | tf_op jit(solution)/shard_map/all_gather | solution.py:126
  305.3 114.8 %reduce-scatter.21.cloned.1.call-start = ((), (), s32[]{:S(2)}) async-start(), calls=%async_computation.13 | async-start | bytes 1966080 | tf_op jit(solution)/shard_map/reduce_scatter | solution.py:187
  333.7 132.5 %copy-start.6 = (f32[2,64,768]{2,1,0:T(8,128)}, f32[2,64,768]{2,1,0:T(8,128)S(1)}, u32[]{:S(2)}) copy-start(f32[2,64,768]{2,1,0:T(8,128)S(1)} %get-tuple-element.395) | copy-start | bytes 1179652
  342.7 9.0 copy-start.12
  351.7 41.8 %copy-start.28 = (bf16[512,768]{1,0:T(8,128)(2,1)}, bf16[512,768]{1,0:T(8,128)(2,1)S(1)}, u32[]{:S(2)}) copy-start(bf16[512,768]{1,0:T(8,128)(2,1)S(1)} %get-tuple-element.416) | copy-start | bytes 2359300
  393.5 26.6 %copy-start.53 = (f32[2,64]{1,0:T(2,128)S(1)}, f32[2,64]{1,0:T(2,128)}, u32[]{:S(2)}) copy-start(f32[2,64]{1,0:T(2,128)} %copy-done.52) | copy-start | bytes 1540
  393.5 26.6 %copy-start.62 = (f32[768]{0:T(1024)S(1)}, f32[768]{0:T(1024)}, u32[]{:S(2)}) copy-start(f32[768]{0:T(1024)} %param.36) | copy-start | bytes 9220
  393.5 26.6 %copy-start.78 = (f32[768]{0:T(1024)S(1)}, f32[768]{0:T(1024)}, u32[]{:S(2)}) copy-start(f32[768]{0:T(1024)} %param.40) | copy-start | bytes 9220
  393.5 28.1 %copy-start.37 = (bf16[2,64,768]{2,1,0:T(8,128)(2,1)S(1)}, bf16[2,64,768]{2,1,0:T(8,128)(2,1)}, u32[]{:S(2)}) copy-start(bf16[2,64,768]{2,1,0:T(8,128)(2,1)} %param.43) | copy-start | bytes 589828
  393.5 28.1 %copy-start.50 = (f32[768]{0:T(1024)S(1)}, f32[768]{0:T(1024)}, u32[]{:S(2)}) copy-start(f32[768]{0:T(1024)} %param.41) | copy-start | bytes 9220
  393.5 69.9 %reduce-scatter.23.cloned.1.call-start = ((), (), s32[]{:S(2)}) async-start(), calls=%async_computation.14 | async-start | bytes 1966080 | tf_op jit(solution)/shard_map/reduce_scatter | solution.py:219
  421.3 8.8 copy-start.82
  421.3 8.8 copy-start.83
  421.3 10.5 %copy-start.58 = (f32[2,64]{1,0:T(2,128)}, f32[2,64]{1,0:T(2,128)S(1)}, u32[]{:S(2)}) copy-start(f32[2,64]{1,0:T(2,128)S(1)} %broadcast_multiply_fusion.10) | copy-start | bytes 1540
  421.6 10.3 %copy-start.63 = (f32[2,64]{1,0:T(2,128)}, f32[2,64]{1,0:T(2,128)S(1)}, u32[]{:S(2)}) copy-start(f32[2,64]{1,0:T(2,128)S(1)} %add_rsqrt_fusion) | copy-start | bytes 1540
  421.8 10.0 copy-start.70
  421.8 10.0 copy-start.72
  434.8 28.7 %copy-start.51 = (f32[768]{0:T(1024)S(1)}, f32[768]{0:T(1024)}, u32[]{:S(2)}) copy-start(f32[768]{0:T(1024)} %param.41) | copy-start | bytes 9220
  434.8 28.7 %copy-start.54 = (f32[2,64]{1,0:T(2,128)S(1)}, f32[2,64]{1,0:T(2,128)}, u32[]{:S(2)}) copy-start(f32[2,64]{1,0:T(2,128)} %copy-done.52) | copy-start | bytes 1540
  434.8 28.7 %copy-start.59 = (f32[2,64]{1,0:T(2,128)S(1)}, f32[2,64]{1,0:T(2,128)}, u32[]{:S(2)}) copy-start(f32[2,64]{1,0:T(2,128)} %copy-done.58) | copy-start | bytes 1540
  434.8 28.7 %copy-start.64 = (f32[2,64]{1,0:T(2,128)S(1)}, f32[2,64]{1,0:T(2,128)}, u32[]{:S(2)}) copy-start(f32[2,64]{1,0:T(2,128)} %copy-done.63) | copy-start | bytes 1540
  434.8 28.7 %copy-start.71 = (f32[2,64]{1,0:T(2,128)S(1)}, f32[2,64]{1,0:T(2,128)}, u32[]{:S(2)}) copy-start(f32[2,64]{1,0:T(2,128)} %copy-done.70) | copy-start | bytes 1540
  434.8 28.7 %copy-start.73 = (f32[2,64]{1,0:T(2,128)S(1)}, f32[2,64]{1,0:T(2,128)}, u32[]{:S(2)}) copy-start(f32[2,64]{1,0:T(2,128)} %copy-done.72) | copy-start | bytes 1540
  434.8 28.7 %copy-start.79 = (f32[768]{0:T(1024)S(1)}, f32[768]{0:T(1024)}, u32[]{:S(2)}) copy-start(f32[768]{0:T(1024)} %param.42) | copy-start | bytes 9220
  434.8 131.8 %all-reduce.5.cloned.1.call-start = ((), (), s32[]{:S(2)}) async-start(), calls=%async_computation.15 | async-start | bytes 3145728 | tf_op jit(solution)/shard_map/psum | solution.py:244
  466.2 9.3 copy-start.20
  466.2 9.3 copy-start.74
  466.2 9.3 copy-start.76
  496.2 161.4 %reduce-scatter.37.cloned.1.call-start = ((), (), s32[]{:S(2)}) async-start(), calls=%async_computation.22 | async-start | bytes 884736
  497.8 7.0 copy-start.10
  497.8 7.0 copy-start.57
  507.3 21.2 %copy-start.23 = (bf16[2,256,768]{2,1,0:T(8,128)(2,1)S(1)}, bf16[2,256,768]{2,1,0:T(8,128)(2,1)}, u32[]{:S(2)}) copy-start(bf16[2,256,768]{2,1,0:T(8,128)(2,1)} %copy-done.22) | copy-start | bytes 2359300
  507.3 21.2 %copy-start.41 = (bf16[24,8,2,256]{3,1,2,0:T(8,128)(2,1)S(1)}, bf16[24,8,2,256]{3,1,2,0:T(8,128)(2,1)}, u32[]{:S(2)}) copy-start(bf16[24,8,2,256]{3,1,2,0:T(8,128)(2,1)} %copy.197) | copy-start | bytes 589828
  507.4 22.5 %copy-start.39 = (f32[2,256,3,64]{1,3,2,0:T(8,128)S(1)}, f32[2,256,3,64]{1,3,2,0:T(8,128)}, u32[]{:S(2)}) copy-start(f32[2,256,3,64]{1,3,2,0:T(8,128)} %get-tuple-element.413) | copy-start | bytes 1179652
  531.0 37.0 %copy-start.33 = (bf16[2,256,3,64]{1,3,2,0:T(8,128)(2,1)}, bf16[2,256,3,64]{1,3,2,0:T(8,128)(2,1)S(1)}, u32[]{:S(2)}) copy-start(bf16[2,256,3,64]{1,3,2,0:T(8,128)(2,1)S(1)} %fusion.96) | copy-start | bytes 589828
  532.6 35.4 %copy-start.9 = (bf16[2,256,3,64]{1,3,2,0:T(8,128)(2,1)S(1)}, bf16[2,256,3,64]{1,3,2,0:T(8,128)(2,1)}, u32[]{:S(2)}) copy-start(bf16[2,256,3,64]{1,3,2,0:T(8,128)(2,1)} %get-tuple-element.797) | copy-start | bytes 589828
  532.7 126.6 %reduce-scatter.25.cloned.1.call-start = ((), (), s32[]{:S(2)}) async-start(), calls=%async_computation.16 | async-start | bytes 983040 | tf_op jit(solution)/shard_map/reduce_scatter | solution.py:270
  568.0 7.5 copy-start.11
  600.1 3.8 copy-start.34
  603.6 121.3 %reduce-scatter.31.cloned.1.call-start = ((), (), s32[]{:S(2)}) async-start(), calls=%async_computation.19 | async-start | bytes 884736
  605.4 192.4 %reduce-scatter.29.cloned.1.call-start = ((), (), s32[]{:S(2)}) async-start(), calls=%async_computation.18 | async-start | bytes 2654208 | tf_op jit(solution)/shard_map/reduce_scatter | solution.py:291
  607.8 263.2 %reduce-scatter.27.cloned.1.call-start = ((), (), s32[]{:S(2)}) async-start(), calls=%async_computation.17 | async-start | bytes 2654208 | tf_op jit(solution)/shard_map/reduce_scatter | solution.py:289
  611.4 325.8 %reduce-scatter.33.cloned.1.call-start = ((), (), s32[]{:S(2)}) async-start(), calls=%async_computation.20 | async-start | bytes 884736
  613.8 389.6 %reduce-scatter.35.cloned.1.call-start = ((), (), s32[]{:S(2)}) async-start(), calls=%async_computation.21 | async-start | bytes 884736
  614.5 44.8 %copy-start.7 = (f32[2,64,768]{2,1,0:T(8,128)S(1)}, f32[2,64,768]{2,1,0:T(8,128)}, u32[]{:S(2)}) copy-start(f32[2,64,768]{2,1,0:T(8,128)} %copy-done.6) | copy-start | bytes 1179652
  614.5 44.8 %copy-start.21 = (f32[2,64,768]{2,1,0:T(8,128)S(1)}, f32[2,64,768]{2,1,0:T(8,128)}, u32[]{:S(2)}) copy-start(f32[2,64,768]{2,1,0:T(8,128)} %copy-done.20) | copy-start | bytes 1179652
  614.5 44.8 %copy-start.55 = (f32[2,64]{1,0:T(2,128)S(1)}, f32[2,64]{1,0:T(2,128)}, u32[]{:S(2)}) copy-start(f32[2,64]{1,0:T(2,128)} %copy-done.52) | copy-start | bytes 1540
  614.5 44.8 %copy-start.75 = (f32[2,64]{1,0:T(2,128)S(1)}, f32[2,64]{1,0:T(2,128)}, u32[]{:S(2)}) copy-start(f32[2,64]{1,0:T(2,128)} %copy-done.74) | copy-start | bytes 1540
  614.5 44.8 %copy-start.77 = (f32[2,64]{1,0:T(2,128)S(1)}, f32[2,64]{1,0:T(2,128)}, u32[]{:S(2)}) copy-start(f32[2,64]{1,0:T(2,128)} %copy-done.76) | copy-start | bytes 1540
  (39 other events, 61.7 us)
Sparse Core Ops, SparseCore 0:
  304.3 28.2 reduce-scatter.18
  393.7 26.3 reduce-scatter.20
  434.9 28.5 reduce-scatter.22
Sparse Core Ops, SparseCore 1:
  306.7 41.7 all-gather.2
  350.4 39.7 all-gather.4
  496.3 70.3 all-reduce.4
  570.0 62.5 reduce-scatter.36
  635.1 22.6 reduce-scatter.24
  661.7 63.1 reduce-scatter.30
  728.8 69.0 reduce-scatter.28
  801.8 69.1 reduce-scatter.26
  874.7 62.4 reduce-scatter.32
  941.1 62.3 reduce-scatter.34
where the time goes:
time: 1020 us; the launch traced here: 1010 us
  waiting for transfers between devices  501 us (49%)
  blocking collectives  320 us (31%)
  local copies, waits for them, and re-layouts  85.6 us (8%)
  matrix products  73.7 us (7%)
  between operations  16.4 us (2%)
  other arithmetic  13 us (1%)
    unnamed x17, waiting for transfers between devices  197 us
    psum x1, blocking collectives, per_device(): kv_sum, z_sum = lax.psum((kv_part, z_part), 'ctx')  96.4 us
    reduce_scatter x1, waiting for transfers between devices, per_device(): lax.psum_scatter(grad_up, ('shard', 'ctx'), scatter_dimension=0, tiled=True)  73.1 us
    reduce_scatter x1, waiting for transfers between devices, per_device(): lax.psum_scatter(grad_down, ('shard', 'ctx'), scatter_dimension=1, tiled=...  73 us
    mul x40, local copies, waits for them, and re-layouts, spread_rows(): wide = mask_low[:, None, :, None] * left[:, :, None, :]  51.8 us
    psum x1, blocking collectives, per_device(): lax.psum((grad_gain_attn, grad_shift_attn, grad_gain_ffn, grad_shift_ffn,...  40.8 us
    all_gather x1, waiting for transfers between devices, per_device(): lax.all_gather(w_down, ('shard', 'ctx'), axis=1, tiled=True)  38.5 us
    psum x1, waiting for transfers between devices, per_device(): lax.psum(kv_grad_part.astype(jnp.bfloat16), 'ctx').astype(jnp.float32)  33.9 us
  transfers between devices with their start and end apart: 13, of which 11 were waited for; matrix products, arithmetic and copies ran while one was open for 7% of the time, Pallas kernels for 0%

commit v1 on v0

--- a/solution.py
+++ b/solution.py
@@ -11,6 +11,18 @@
 root_half = 0.7071067811865476
 inv_root_tau = 0.3989422804014327
 norm_eps = 1e-05
+
+
+def collect(x, axis, dim):
+    ways, here = (lax.axis_size(axis), lax.axis_index(axis))
+    grown, reach = (x, 1)
+    while reach < ways:
+        theirs = lax.ppermute(grown, axis, [(d, d ^ reach) for d in range(ways)])
+        mine_first = jnp.concatenate([grown, theirs], axis=dim)
+        theirs_first = jnp.concatenate([theirs, grown], axis=dim)
+        grown = jnp.where(here & reach == 0, mine_first, theirs_first)
+        reach = 2 * reach
+    return grown
 
 
 def gelu_value(upper):
@@ -122,7 +134,7 @@
         lax.all_gather(w_key, ("shard", "ctx"), axis=0, tiled=True),
         lax.all_gather(w_value, ("shard", "ctx"), axis=0, tiled=True),
         lax.all_gather(w_up, ("shard", "ctx"), axis=0, tiled=True),
-        lax.all_gather(w_out, ("shard", "ctx"), axis=1, tiled=True),
+        collect(w_out, ("shard", "ctx"), 1),
         lax.all_gather(w_down, ("shard", "ctx"), axis=1, tiled=True),
     )
     seq_count, row_share, width = inputs.shape

time: 1020 us -> 989 us (0.970)
  waiting for transfers between devices: 501 us -> 453 us
  local copies, waits for them, and re-layouts: 85.6 us -> 96.5 us
    reduce_scatter x4 -> x0, waiting for transfers between devices: 79.2 us -> none  [the longest x1 27.2 us: per_device(): lax.psum_scatter(jnp.einsum('scf,fd->csd', piece, full_out, preferred_ele...]
    unnamed x17 -> x21, waiting for transfers between devices: 197 us -> 234 us
    all_gather x1, waiting for transfers between devices: 38.5 us -> 26.5 us  [per_device(): lax.all_gather(w_down, ('shard', 'ctx'), axis=1, tiled=True)]
  transfers between devices with their start and end apart: 13 -> 16, of which waited for: 11 -> 12; matrix products, arithmetic and copies ran while one was open for 7% -> 13% of each run, Pallas kernels for 0% -> 0%
where the time goes in v1:
time: 989 us; the launch traced here: 981 us
  waiting for transfers between devices  453 us (46%)
  blocking collectives  319 us (32%)
  local copies, waits for them, and re-layouts  96.5 us (10%)
  matrix products  69.3 us (7%)
  other arithmetic  20.5 us (2%)
  between operations  16.9 us (2%)
    unnamed x21, waiting for transfers between devices  234 us
    psum x1, blocking collectives, per_device(): kv_sum, z_sum = lax.psum((kv_part, z_part), 'ctx')  96.9 us
    reduce_scatter x1, waiting for transfers between devices, per_device(): lax.psum_scatter(grad_up, ('shard', 'ctx'), scatter_dimension=0, tiled=True)  73 us
    reduce_scatter x1, waiting for transfers between devices, per_device(): lax.psum_scatter(grad_down, ('shard', 'ctx'), scatter_dimension=1, tiled=...  73 us
    mul x40, local copies, waits for them, and re-layouts, spread_rows(): wide = mask_low[:, None, :, None] * left[:, :, None, :]  51.4 us
    psum x1, blocking collectives, per_device(): lax.psum((grad_gain_attn, grad_shift_attn, grad_gain_ffn, grad_shift_ffn,...  40.6 us
    psum x1, waiting for transfers between devices, per_device(): lax.psum(kv_grad_part.astype(jnp.bfloat16), 'ctx').astype(jnp.float32)  37.1 us
    all_gather x1, blocking collectives, per_device(): lax.all_gather(w_key, ('shard', 'ctx'), axis=0, tiled=True)  32.2 us
  transfers between devices with their start and end apart: 16, of which 12 were waited for; matrix products, arithmetic and copies ran while one was open for 13% of the time, Pallas kernels for 0%

profile of v1, /device:TPU:0, one launch (start us, length us, event | category | flops | bytes accessed | tf_op | source)
XLA Modules:
  0.0 980.7 jit_solution(13319040716567500279)
XLA Ops:
  8.1 3.1 collective-permute-start
  11.2 8.8 all_gather.35
  20.0 32.2 %all_gather.36 = bf16[768,192]{1,0:T(8,128)(2,1)S(1)} all-gather(bf16[96,192]{1,0:T(8,128)(2,1)} %param.32), channel_id=1, replica_groups=mesh['shard'=2,'ctx'=4,'tp'=4] {'shard','ctx'}, dimensions={0}, use_global_device_ids=true | all-gather | bytes 331776 | tf_op jit(solution)/shard_map/all_gather | solution.py:134
  53.6 2.7 fusion.171
  57.5 31.7 %all_gather.37 = bf16[768,192]{1,0:T(8,128)(2,1)S(1)} all-gather(bf16[96,192]{1,0:T(8,128)(2,1)S(1)} %copy-done.46), channel_id=1, replica_groups=mesh['shard'=2,'ctx'=4,'tp'=4] {'shard','ctx'}, dimensions={0}, use_global_device_ids=true | all-gather | bytes 331776 | tf_op jit(solution)/shard_map/all_gather | solution.py:135
  92.0 2.1 convolution_bitcast_fusion.8
  94.0 20.6 %while.66 = (s32[]{:T(128)}, f32[2,3,2048,64]{2,3,1,0:T(8,128)}, bf16[2,256,8]{2,1,0:T(8,128)(2,1)S(1)}, bf16[2,256,3,256]{3,1,2,0:T(8,128)(2,1)}, bf16[2,256,3,64]{1,3,2,0:T(8,128)(2,1)}) while((s32[]{:T(128)}, f32[2,3,2048,64]{2,3,1,0:T(8,128)}, bf16[2,256,8]{2,1,0:T(8,128)(2,1)S(1)}, bf16[2,256,3,256]{3,1,2,0:T(8,128)(2,1)}, ...), condition=%wide.region_3.4_spmd.clone, body=%wide.region_2.3_spmd.sunk.clone | while | flops 207618048 | bytes 20427872 | solution.py:163
  95.1 2.1 mul.672
  97.2 4.2 mul.673
  102.3 2.0 fusion.245
  105.4 2.1 mul.672
  107.5 4.2 mul.673
  114.7 32.0 %all_gather.38 = bf16[768,192]{1,0:T(8,128)(2,1)S(1)} all-gather(bf16[96,192]{1,0:T(8,128)(2,1)S(1)} %copy-done.47), channel_id=1, replica_groups=mesh['shard'=2,'ctx'=4,'tp'=4] {'shard','ctx'}, dimensions={0}, use_global_device_ids=true | all-gather | bytes 331776 | tf_op jit(solution)/shard_map/all_gather | solution.py:133
  146.8 2.3 broadcast_multiply_fusion
  149.1 2.7 fusion.172
  153.1 96.9 %all-reduce.22 = (bf16[2,3,2048,64]{2,3,1,0:T(8,128)(2,1)}, f32[2,3,8,256]{3,2,1,0:T(8,128)S(1)}) all-reduce(f32[2,3,2048,64]{2,3,1,0:T(8,128)} %get-tuple-element.176, f32[2,3,8,256]{3,2,1,0:T(8,128)S(1)} %copy-done.44), channel_id=1, replica_groups=mesh['shard'=2,'ctx'=4,'tp'=4] {'ctx'}, use_global_device_ids=true, to_apply=%region_4.5 | all-reduce | flops 798720 | bytes 4816896 | tf_op jit(solution)/shard_map/psum | solution.py:165
  250.0 19.2 %while.67 = (s32[]{:T(128)}, f32[2,256,3,64]{1,3,2,0:T(8,128)}, bf16[2,3,2048,64]{2,3,1,0:T(8,128)(2,1)}, bf16[2,256,8]{2,1,0:T(8,128)(2,1)S(1)}, bf16[2,256,3,256]{3,1,2,0:T(8,128)(2,1)}) while((s32[]{:T(128)}, f32[2,256,3,64]{1,3,2,0:T(8,128)}, bf16[2,3,2048,64]{2,3,1,0:T(8,128)(2,1)}, bf16[2,256,8]{2,1,0:T(8,128)(2,1)S(1)}, ...), condition=%wide.region_6.7_spmd.clone, body=%wide.region_5.6_spmd.sunk.clone | while | flops 202899456 | bytes 31536224 | solution.py:167
  251.4 3.4 mul.678
  256.7 2.9 fusion.248
  261.1 3.4 mul.678
  266.3 2.8 fusion.248
  273.9 4.0 collective-permute-done.1
  278.2 5.1 collective-permute-done.2
  283.7 2.2 copy.129
  288.4 39.0 %all-reduce.15.cloned.1.call-done = f32[256,2,768]{2,1,0:T(2,128)} async-done(((f32[256,2,768]{2,1,0:T(2,128)}), f32[256,2,768]{2,1,0:T(2,128)}) %all-reduce.15.cloned.1.call-update) | async-done | bytes 1572880
  331.6 8.1 all_gather.39
  339.8 3.5 multiply_convert_fusion
  343.4 26.5 %all-gather.5.cloned.1.call-done = bf16[768,768]{0,1:T(8,128)(2,1)} async-done(((bf16[768,96]{0,1:T(8,128)(2,1)}), bf16[768,768]{0,1:T(8,128)(2,1)}) %all-gather.5.cloned.1.call-update) | async-done | bytes 1179664 | tf_op jit(solution)/shard_map/all_gather | solution.py:138
  369.9 2.1 convolution_bitcast_fusion.2
  372.0 2.5 copy.131
  374.5 41.3 %all-reduce.17.cloned.1.call-done = f32[256,2,768]{2,1,0:T(2,128)} async-done(((f32[256,2,768]{2,1,0:T(2,128)}), f32[256,2,768]{2,1,0:T(2,128)}) %all-reduce.17.cloned.1.call-update) | async-done | bytes 1572880
  421.3 8.4 all_gather.42
  433.2 2.4 copy.134
  437.1 32.0 %all_gather.44 = bf16[192,768]{0,1:T(8,128)(2,1)S(1)} all-gather(bf16[192,96]{0,1:T(8,128)(2,1)S(1)} %copy.135), channel_id=1, replica_groups=mesh['shard'=2,'ctx'=4,'tp'=4] {'shard','ctx'}, dimensions={1}, use_global_device_ids=true | all-gather | bytes 331776 | tf_op jit(solution)/shard_map/all_gather | solution.py:215
  471.3 7.8 all-reduce.19.cloned.1.call-done
  479.1 2.3 multiply_reduce_fusion.2
  482.6 8.2 all_gather.43
  492.9 20.1 %while.69 = (s32[]{:T(128)}, bf16[2,3,2048,64]{2,3,1,0:T(8,128)(2,1)}, bf16[2,256,8]{2,1,0:T(8,128)(2,1)S(1)}, bf16[2,256,3,256]{3,1,2,0:T(8,128)(2,1)}, bf16[2,256,3,64]{1,3,2,0:T(8,128)(2,1)}) while((s32[]{:T(128)}, bf16[2,3,2048,64]{2,3,1,0:T(8,128)(2,1)}, bf16[2,256,8]{2,1,0:T(8,128)(2,1)S(1)}, ...), condition=%wide.region_26.27_spmd.clone, body=%wide.region_25.26_spmd.sunk.clone | while | flops 207618048 | bytes 20427872 | solution.py:251
  494.0 2.1 mul.684
  496.0 4.2 mul.685
  504.0 2.1 mul.684
  506.1 4.2 mul.685
  514.9 7.0 while.68
  514.9 2.0 fusion.251
  521.9 2.5 fusion.173
  525.5 20.6 %psum.73 = bf16[2,3,8,256]{3,2,1,0:T(8,128)(2,1)S(1)} all-reduce(bf16[2,3,8,256]{3,2,1,0:T(8,128)(2,1)S(1)} %fusion.107), channel_id=1, replica_groups=mesh['shard'=2,'ctx'=4,'tp'=4] {'ctx'}, use_global_device_ids=true, to_apply=%region_31.32 | all-reduce | flops 12288 | bytes 49152 | tf_op jit(solution)/shard_map/psum | solution.py:257
  550.2 37.1 %all-reduce.13.cloned.1.call-done = bf16[2,3,2048,64]{2,3,1,0:T(8,128)(2,1)} async-done(((bf16[2,3,2048,64]{2,3,1,0:T(8,128)(2,1)}), bf16[2,3,2048,64]{2,3,1,0:T(8,128)(2,1)}) %all-reduce.13.cloned.1.call-update) | async-done | bytes 1572880 | tf_op jit(solution)/shard_map/psum | solution.py:256
  588.6 7.5 while.70
  588.6 2.3 fusion.257
  592.4 2.2 fusion.257
  600.9 19.5 %while.71 = (s32[]{:T(128)}, bf16[2,256,3,64]{1,3,2,0:T(8,128)(2,1)}, bf16[2,3,2048,64]{2,3,1,0:T(8,128)(2,1)}, bf16[2,256,8]{2,1,0:T(8,128)(2,1)S(1)}, bf16[2,256,3,256]{3,1,2,0:T(8,128)(2,1)}) while((s32[]{:T(128)}, bf16[2,256,3,64]{1,3,2,0:T(8,128)(2,1)}, bf16[2,3,2048,64]{2,3,1,0:T(8,128)(2,1)}, ...), condition=%wide.region_34.35_spmd.clone, body=%wide.region_33.34_spmd.sunk.clone | while | flops 202899456 | bytes 33109144 | solution.py:266
  602.4 3.4 mul.692
  607.8 2.2 fusion.260
  612.1 3.4 mul.692
  617.5 2.2 fusion.260
  620.4 2.5 fusion.75
  629.8 2.3 fusion.176
  633.5 2.2 fusion.175
  637.6 40.6 %all-reduce.4 = (f32[768]{0:T(1024)}, f32[768]{0:T(1024)}, f32[3072]{0:T(1024)S(1)}, f32[768]{0:T(1024)}, f32[768]{0:T(1024)}, /*index=5*/f32[768]{0:T(1024)}) all-reduce(f32[768]{0:T(1024)S(1)} %copy-done.54, f32[768]{0:T(1024)S(1)} %copy-done.55, ...), channel_id=1, replica_groups=mesh['shard'=2,'ctx'=4,'tp'=4] {'shard','ctx','tp'}, use_global_device_ids=true, to_apply=%region_41.42 | all-reduce | flops 6912 | bytes 55296 | tf_op jit(solution)/shard_map/psum | solution.py:310
  682.3 12.6 %reduce-scatter.19.cloned.1.call-done = f32[96,192]{1,0:T(8,128)} async-done(((f32[768,192]{1,0:T(8,128)}), f32[96,192]{1,0:T(8,128)}) %reduce-scatter.19.cloned.1.call-update) | async-done | bytes 73744
  694.8 66.3 %reduce-scatter.21.cloned.1.call-done = f32[96,192]{1,0:T(8,128)} async-done(((f32[768,192]{1,0:T(8,128)}), f32[96,192]{1,0:T(8,128)}) %reduce-scatter.21.cloned.1.call-update) | async-done | bytes 73744
  761.1 66.3 %reduce-scatter.23.cloned.1.call-done = f32[96,192]{1,0:T(8,128)} async-done(((f32[768,192]{1,0:T(8,128)}), f32[96,192]{1,0:T(8,128)}) %reduce-scatter.23.cloned.1.call-update) | async-done | bytes 73744
  827.4 73.0 %reduce-scatter.17.cloned.1.call-done = f32[768,96]{0,1:T(8,128)} async-done(((f32[768,768]{0,1:T(8,128)}), f32[768,96]{0,1:T(8,128)}) %reduce-scatter.17.cloned.1.call-update) | async-done | bytes 294928 | tf_op jit(solution)/shard_map/reduce_scatter | solution.py:303
  900.3 73.0 %reduce-scatter.15.cloned.1.call-done = f32[96,768]{1,0:T(8,128)} async-done(((f32[768,768]{1,0:T(8,128)}), f32[96,768]{1,0:T(8,128)}) %reduce-scatter.15.cloned.1.call-update) | async-done | bytes 294928 | tf_op jit(solution)/shard_map/reduce_scatter | solution.py:301
  (305 shorter events, 97.3 us)
Async XLA Ops:
  8.0 45.5 %copy-start = (f32[3,64,256]{2,1,0:T(8,128)S(1)}, f32[3,64,256]{2,1,0:T(8,128)}, u32[]{:S(2)}) copy-start(f32[3,64,256]{2,1,0:T(8,128)} %param.30) | copy-start | bytes 589828
  8.0 319.3 %all-reduce.15.cloned.1.call-start = ((), (), s32[]{:S(2)}) async-start(), calls=%async_computation.15 | async-start | bytes 3145728
  8.1 262.2 %collective-permute-start = (bf16[192,96]{1,0:T(8,128)(2,1)}, bf16[192,96]{1,0:T(8,128)(2,1)}, u32[]{:S(2)}, u32[]{:S(2)}) collective-permute-start(bf16[192,96]{1,0:T(8,128)(2,1)} %param.34), channel_id=1, source_target_pairs={{0,4},{4,0},{8,12},{12,8},{16,20},{20,16},{24,28},{28,24},{1,5},{5... | collective-permute-start | bytes 110600 | tf_op jit(solution)/shard_map/ppermute | solution.py:20
  20.0 69.2 %copy-start.4 = (bf16[2,256,768]{2,1,0:T(8,128)(2,1)}, bf16[2,256,768]{2,1,0:T(8,128)(2,1)S(1)}, u32[]{:S(2)}) copy-start(bf16[2,256,768]{2,1,0:T(8,128)(2,1)S(1)} %all_gather.35) | copy-start | bytes 2359300
  52.2 4.1 copy-start.14
  53.6 4.0 copy-start.46
  57.5 33.6 %copy-start.48 = (s32[2,256]{1,0:T(2,128)S(1)}, s32[2,256]{1,0:T(2,128)}, u32[]{:S(2)}) copy-start(s32[2,256]{1,0:T(2,128)} %param.29) | copy-start | bytes 6148
  94.0 20.6 %copy-start.47 = (bf16[96,192]{1,0:T(8,128)(2,1)S(1)}, bf16[96,192]{1,0:T(8,128)(2,1)}, u32[]{:S(2)}) copy-start(bf16[96,192]{1,0:T(8,128)(2,1)} %param.31) | copy-start | bytes 110596
  146.7 5.2 copy-start.16
  149.1 3.9 copy-start.44
  151.9 98.1 %copy-start.19 = (bf16[2,256,3,256]{1,3,0,2:T(8,128)(2,1)}, bf16[2,256,3,256]{1,3,0,2:T(8,128)(2,1)S(1)}, u32[]{:S(2)}) copy-start(bf16[2,256,3,256]{1,3,0,2:T(8,128)(2,1)S(1)} %get-tuple-element.412) | copy-start | bytes 2359300
  254.8 1.9 copy-start.1
  264.5 1.9 copy-start.1
  269.2 9.0 copy-start.41
  271.3 6.6 collective-permute-start.1
  278.1 5.2 collective-permute-start.2
  285.9 41.5 %copy-start.21 = (bf16[2,64,768]{2,1,0:T(8,128)(2,1)S(1)}, bf16[2,64,768]{2,1,0:T(8,128)(2,1)}, u32[]{:S(2)}) copy-start(bf16[2,64,768]{2,1,0:T(8,128)(2,1)} %param.28) | copy-start | bytes 589828
  285.9 44.2 %copy-start.45 = (f32[768]{0:T(1024)S(1)}, f32[768]{0:T(1024)}, u32[]{:S(2)}) copy-start(f32[768]{0:T(1024)} %param.35) | copy-start | bytes 9220
  285.9 44.2 %copy-start.49 = (f32[768]{0:T(1024)S(1)}, f32[768]{0:T(1024)}, u32[]{:S(2)}) copy-start(f32[768]{0:T(1024)} %param.36) | copy-start | bytes 9220
  285.9 53.9 %all-gather.3.cloned.1.call-start = ((), (), s32[]{:S(2)}) async-start(), calls=%async_computation.6 | async-start | bytes 1327104 | tf_op jit(solution)/shard_map/all_gather | solution.py:136
  286.5 83.4 %all-gather.5.cloned.1.call-start = ((), (), s32[]{:S(2)}) async-start(), calls=%async_computation.7 | async-start | bytes 1327104 | tf_op jit(solution)/shard_map/all_gather | solution.py:138
  287.1 128.8 %all-reduce.17.cloned.1.call-start = ((), (), s32[]{:S(2)}) async-start(), calls=%async_computation.16 | async-start | bytes 3145728
  331.6 8.2 copy-start.61
  339.8 3.6 copy-start.10
  343.4 28.6 %copy-start.24 = (bf16[512,768]{1,0:T(8,128)(2,1)}, bf16[512,768]{1,0:T(8,128)(2,1)S(1)}, u32[]{:S(2)}) copy-start(bf16[512,768]{1,0:T(8,128)(2,1)S(1)} %get-tuple-element.414) | copy-start | bytes 2359300
  374.4 41.4 %copy-start.56 = (f32[768]{0:T(1024)S(1)}, f32[768]{0:T(1024)}, u32[]{:S(2)}) copy-start(f32[768]{0:T(1024)} %param.40) | copy-start | bytes 9220
  374.4 43.2 %copy-start.38 = (bf16[2,64,768]{2,1,0:T(8,128)(2,1)S(1)}, bf16[2,64,768]{2,1,0:T(8,128)(2,1)}, u32[]{:S(2)}) copy-start(bf16[2,64,768]{2,1,0:T(8,128)(2,1)} %param.43) | copy-start | bytes 589828
  374.4 43.2 %copy-start.50 = (f32[768]{0:T(1024)S(1)}, f32[768]{0:T(1024)}, u32[]{:S(2)}) copy-start(f32[768]{0:T(1024)} %param.41) | copy-start | bytes 9220
  374.5 44.7 %copy-start.57 = (f32[768]{0:T(1024)S(1)}, f32[768]{0:T(1024)}, u32[]{:S(2)}) copy-start(f32[768]{0:T(1024)} %param.42) | copy-start | bytes 9220
  374.5 104.6 %all-reduce.19.cloned.1.call-start = ((), (), s32[]{:S(2)}) async-start(), calls=%async_computation.17 | async-start | bytes 3145728
  421.1 8.6 copy-start.60
  421.1 8.6 copy-start.63
  429.7 1.7 copy-start.22
  429.8 2.6 copy-start.59
  435.6 151.7 %all-reduce.13.cloned.1.call-start = ((), (), s32[]{:S(2)}) async-start(), calls=%async_computation.8 | async-start | bytes 3145728 | tf_op jit(solution)/shard_map/psum | solution.py:256
  482.6 9.2 copy-start.42
  513.0 2.0 copy-start.3
  513.0 165.8 %reduce-scatter.25.cloned.1.call-start = ((), (), s32[]{:S(2)}) async-start(), calls=%async_computation.14 | async-start | bytes 884736
  514.9 7.0 copy-start.8
  521.9 2.6 copy-start.20
  524.5 21.6 %copy-start.18 = (bf16[2,256,768]{2,1,0:T(8,128)(2,1)S(1)}, bf16[2,256,768]{2,1,0:T(8,128)(2,1)}, u32[]{:S(2)}) copy-start(bf16[2,256,768]{2,1,0:T(8,128)(2,1)} %copy.159) | copy-start | bytes 2359300
  524.5 21.6 %copy-start.37 = (bf16[24,8,2,256]{3,1,2,0:T(8,128)(2,1)S(1)}, bf16[24,8,2,256]{3,1,2,0:T(8,128)(2,1)}, u32[]{:S(2)}) copy-start(bf16[24,8,2,256]{3,1,2,0:T(8,128)(2,1)} %copy.231) | copy-start | bytes 589828
  524.5 22.9 %copy-start.34 = (f32[2,256,3,64]{1,3,2,0:T(8,128)S(1)}, f32[2,256,3,64]{1,3,2,0:T(8,128)}, u32[]{:S(2)}) copy-start(f32[2,256,3,64]{1,3,2,0:T(8,128)} %get-tuple-element.411) | copy-start | bytes 1179652
  548.6 40.1 %copy-start.29 = (bf16[2,256,3,64]{1,3,2,0:T(8,128)(2,1)}, bf16[2,256,3,64]{1,3,2,0:T(8,128)(2,1)S(1)}, u32[]{:S(2)}) copy-start(bf16[2,256,3,64]{1,3,2,0:T(8,128)(2,1)S(1)} %fusion.96) | copy-start | bytes 589828
  550.2 38.5 %copy-start.7 = (bf16[2,256,3,64]{1,3,2,0:T(8,128)(2,1)S(1)}, bf16[2,256,3,64]{1,3,2,0:T(8,128)(2,1)}, u32[]{:S(2)}) copy-start(bf16[2,256,3,64]{1,3,2,0:T(8,128)(2,1)} %get-tuple-element.795) | copy-start | bytes 589828
  550.2 130.2 %all-reduce.21.cloned.1.call-start = ((), (), s32[]{:S(2)}) async-start(), calls=%async_computation.18 | async-start | bytes 1572864
  588.6 7.5 copy-start.9
  596.1 2.0 copy-start.33
  605.8 2.0 copy-start.2
  615.5 2.0 copy-start.2
  623.0 1.8 copy-start.5
  623.0 1.8 copy-start.30
  624.7 1.7 copy-start.32
  624.7 70.1 %reduce-scatter.19.cloned.1.call-start = ((), (), s32[]{:S(2)}) async-start(), calls=%async_computation.11 | async-start | bytes 884736
  626.3 134.8 %reduce-scatter.21.cloned.1.call-start = ((), (), s32[]{:S(2)}) async-start(), calls=%async_computation.12 | async-start | bytes 884736
  627.9 199.5 %reduce-scatter.23.cloned.1.call-start = ((), (), s32[]{:S(2)}) async-start(), calls=%async_computation.13 | async-start | bytes 884736
  629.7 270.6 %reduce-scatter.17.cloned.1.call-start = ((), (), s32[]{:S(2)}) async-start(), calls=%async_computation.10 | async-start | bytes 2654208 | tf_op jit(solution)/shard_map/reduce_scatter | solution.py:303
  632.1 341.2 %reduce-scatter.15.cloned.1.call-start = ((), (), s32[]{:S(2)}) async-start(), calls=%async_computation.9 | async-start | bytes 2654208 | tf_op jit(solution)/shard_map/reduce_scatter | solution.py:301
  635.7 1.8 copy-start.51
  635.7 1.8 copy-start.52
  635.7 1.8 copy-start.53
  635.7 1.8 copy-start.54
  635.7 1.8 copy-start.55
  635.7 44.7 %copy-start.35 = (f32[2,64,768]{2,0,1:T(2,128)S(1)}, f32[2,64,768]{2,0,1:T(2,128)}, u32[]{:S(2)}) copy-start(f32[2,64,768]{2,0,1:T(2,128)} %get-tuple-element.393) | copy-start | bytes 1179652
  (22 other events, 24.5 us)
Sparse Core Ops, SparseCore 0:
  286.0 41.2 all-reduce.14
  374.6 41.2 all-reduce.16
  435.7 43.3 all-reduce.18
  513.1 74.1 all-reduce.12
  624.8 34.0 all-reduce.20
Sparse Core Ops, SparseCore 1:
  288.5 39.6 all-gather.2
  330.1 39.7 all-gather.4
  550.3 78.1 reduce-scatter.24
  632.4 62.4 reduce-scatter.18
  698.7 62.4 reduce-scatter.20
  765.0 62.3 reduce-scatter.22
  831.3 69.0 reduce-scatter.16
  904.2 69.0 reduce-scatter.14
